TPU v7x, 32 devices: a whole 2x2x4 slice. The times are simulated.
32 devices in a mesh: layer: 8 (over z, x), tile: 4 (over y, core).
Axes of the slice: x: 2, y: 2, z: 4, core: 2. Of those that a mesh axis runs over, the one named last changes fastest.
Arguments:
- source_modes: bfloat16 [8, 8, 2, 32, 512], P('layer', None, None, 'tile'), may hold values from -6 to 6
- port_cells: int32 [8], replicated, may hold values from 0 to 511
- frequencies: float32 [2], replicated, may hold values from 0.3 to 1.5, as said below
- layer_inverse: bfloat16 [8, 2, 32, 512, 512], P('layer', None, 'tile'), may hold values from -0.092807765 to 1.6928078
- coupling_self: float32 [8, 2, 32, 512], P('layer', None, 'tile'), may hold values from 0.4 to 1
- coupling_curl: float32 [8, 2, 32, 512], P('layer', None, 'tile'), may hold values from -4 to 4
Outputs:
- snapshot_basis: float32 [8, 32, 2, 32, 512], P('layer', None, None, 'tile')
- triangle: float32 [32, 32], replicated
Inputs may be any that keep to these rules, and one draw needn't show every extreme that they name: `port_cells`: each port's profile is centred on this plane column. `frequencies`: the second frequency is 1.5 to 2.5 times the first.
All inputs are finite; a program needn't handle non-finite values.
Results may differ from a plain program's by a relative error of at most 0.04.
Values may be sent and summed in bfloat16 or wider, within the bound.
A program may use at most 64 MiB of HBM per device.

v0:
```python
import jax
import jax.numpy as jnp
from jax import lax
from jax.sharding import PartitionSpec as P


def with_halo(cells, sides, width):
    for axis, dim in sides:
        count = lax.axis_size(axis)
        ends = count - 1
        head = lax.slice_in_dim(cells, 0, width, axis=dim)
        tail = lax.slice_in_dim(cells, cells.shape[dim] - width, cells.shape[dim], axis=dim)
        cells = jnp.concatenate(
            [
                lax.ppermute(tail, axis, [(i, (i + 1) % count) for i in range(ends)]),
                cells,
                lax.ppermute(head, axis, [((i + 1) % count, i) for i in range(ends)]),
            ],
            axis=dim,
        )
    return cells


def shifted(array, axis, by):
    size = lax.axis_size(axis)
    pairs = [(i, i + by) for i in range(size) if 0 <= i + by < size]
    return lax.ppermute(array, axis, pairs)


def lower_factor(gram):
    order = gram.shape[0]
    index_row = jnp.arange(order)

    def column_step(col_no, lower):
        unit = (index_row == col_no).astype(gram.dtype)
        column = jnp.dot(gram, unit, precision=lax.Precision.HIGHEST)
        lower_row = jnp.dot(unit, lower, precision=lax.Precision.HIGHEST)
        column = column - jnp.dot(lower, lower_row, precision=lax.Precision.HIGHEST)
        pivot = jnp.sqrt(jnp.sum(column * unit))
        scaled = jnp.where(index_row >= col_no, column / pivot, 0.0)
        return lower + scaled[:, None] * unit[None, :]

    return lax.fori_loop(0, order, column_step, jnp.zeros_like(gram))


def lower_inverse(lower):
    order = lower.shape[0]
    index_row = jnp.arange(order)

    def row_step(row_no, inverse):
        unit = (index_row == row_no).astype(lower.dtype)
        lower_row = jnp.dot(unit, lower, precision=lax.Precision.HIGHEST)
        pivot = jnp.sum(lower_row * unit)
        new_row = (unit - jnp.dot(lower_row, inverse, precision=lax.Precision.HIGHEST)) / pivot
        return inverse + unit[:, None] * new_row[None, :]

    return lax.fori_loop(0, order, row_step, jnp.zeros_like(lower))


def per_device(source_modes, port_cells, frequencies, layer_inverse, coupling_self, coupling_curl):
    layers_total = lax.axis_size("layer")
    tile_count = lax.axis_size("tile")
    layer_pos = lax.axis_index("layer")
    inverse_block = layer_inverse[0]
    self_w = coupling_self[0]
    curl_w = coupling_curl[0]
    rows_dev = source_modes.shape[3]
    plane_width = source_modes.shape[4]
    columns = jnp.arange(plane_width, dtype=jnp.float32)
    offsets = (columns[None, :] - port_cells.astype(jnp.float32)[:, None]) / (plane_width // 8)
    port_taper = 1.0 / (1.0 + offsets * offsets)
    phase_angle = frequencies * (layer_pos + 1).astype(jnp.float32)
    phase_pair = jnp.stack([jnp.cos(phase_angle), jnp.sin(phase_angle)], axis=1)
    source_layer = source_modes[0].astype(jnp.float32)
    forcing = (
        source_layer[:, None, None]
        * port_taper[:, None, None, None, None, :]
        * phase_pair[None, :, :, None, None, None]
    )
    forcing = forcing.reshape((-1, 2, rows_dev, plane_width))
    column_total = forcing.shape[0]
    group_count = 4
    group_width = column_total // group_count
    forcing_groups = forcing.reshape(group_count, group_width, 2, rows_dev, plane_width)
    step_count = layers_total + group_count - 1

    def couple(field):
        x_part = field[:, 0].astype(jnp.float32)
        y_part = field[:, 1].astype(jnp.float32)
        rim_rows = with_halo(y_part, (("tile", 1),), 1)
        row_diff = rim_rows[:, 2:] - rim_rows[:, :-2]
        cols_pad = jnp.pad(x_part, ((0, 0), (0, 0), (1, 1)))
        col_diff = cols_pad[:, :, 2:] - cols_pad[:, :, :-2]
        part_one = self_w[0] * x_part + curl_w[0] * row_diff
        part_two = self_w[1] * y_part + curl_w[1] * col_diff
        return jnp.stack([part_one, part_two], axis=1)

    def apply_inverse(vectors):
        return jnp.einsum(
            "crik,jcrk->jcri", inverse_block, vectors, preferred_element_type=jnp.float32
        )

    store_shape = (group_count, group_width, 2, rows_dev, plane_width)
    group_shape = (group_width, 2, rows_dev, plane_width)

    def down_step(step_no, state_pair):
        stored, incoming = state_pair
        group_no = jnp.clip(step_no - layer_pos, 0, group_count - 1)
        forcing_now = lax.dynamic_index_in_dim(forcing_groups, group_no, 0, keepdims=False)
        residue = (forcing_now - couple(incoming)).astype(jnp.bfloat16)
        current = apply_inverse(residue).astype(jnp.bfloat16)
        stored = lax.dynamic_update_index_in_dim(stored, current, group_no, 0)
        incoming = shifted(current, "layer", 1)
        return (stored, incoming)

    down_store, _ = lax.fori_loop(
        0,
        step_count,
        down_step,
        (jnp.zeros(store_shape, jnp.bfloat16), jnp.zeros(group_shape, jnp.bfloat16)),
    )
    reverse_pos = layers_total - 1 - layer_pos

    def up_step(step_no, state_pair):
        stored, incoming = state_pair
        group_no = jnp.clip(step_no - reverse_pos, 0, group_count - 1)
        earlier = lax.dynamic_index_in_dim(down_store, group_no, 0, keepdims=False)
        up_image = couple(incoming).astype(jnp.bfloat16)
        current = earlier.astype(jnp.float32) - apply_inverse(up_image)
        stored = lax.dynamic_update_index_in_dim(stored, current, group_no, 0)
        incoming = shifted(current, "layer", -1)
        return (stored, incoming)

    up_store, _ = lax.fori_loop(
        0,
        step_count,
        up_step,
        (jnp.zeros(store_shape, jnp.float32), jnp.zeros(group_shape, jnp.float32)),
    )
    columns_mat = up_store.reshape(column_total, -1)
    gram_local = jnp.dot(columns_mat, columns_mat.T, precision=lax.Precision.HIGHEST)
    total_rows = layers_total * tile_count * columns_mat.shape[1]
    gram_whole = lax.psum(gram_local, ("layer", "tile"))
    triangle = lower_factor(gram_whole / total_rows).T
    solved = jnp.dot(lower_inverse(triangle.T), columns_mat, precision=lax.Precision.HIGHEST)
    basis_out = solved.reshape(1, column_total, 2, rows_dev, plane_width)
    return (basis_out, triangle)


def solution(mesh):
    in_specs = (
        P("layer", None, None, "tile", None),
        P(),
        P(),
        P("layer", None, "tile", None, None),
        P("layer", None, "tile", None),
        P("layer", None, "tile", None),
    )
    out_specs = (P("layer", None, None, "tile", None), P())
    return jax.shard_map(
        per_device, mesh=mesh, in_specs=in_specs, out_specs=out_specs, check_vma=False
    )
```

profile of v0, /device:TPU:0, one launch (start us, length us, event | category | flops | bytes accessed | tf_op | source)
XLA Modules:
  0.0 634.1 jit_solution(17380595981949021285)
XLA Ops:
  3.6 223.6 %while.63 = (s32[]{:T(128)}, bf16[4,8,2,8,512]{4,1,3,2,0:T(8,128)(2,1)S(1)}, bf16[8,2,8,512]{3,0,2,1:T(8,128)(2,1)S(1)}, s32[]{:T(128)}, f32[4,8,2,8,512]{4,3,2,...) while((s32[]{:T(128)}, ...), condition=%wide.region_1.2_spmd, body=%wide.region_0.1_spmd.sunk | while | flops 67829760 | bytes 11698449 | solution.py:116
  11.4 5.7 bitcast_dynamic-update-slice_fusion.4
  30.1 5.7 bitcast_dynamic-update-slice_fusion.4
  49.8 5.7 bitcast_dynamic-update-slice_fusion.4
  69.5 5.7 bitcast_dynamic-update-slice_fusion.4
  90.1 5.7 bitcast_dynamic-update-slice_fusion.4
  131.3 5.7 bitcast_dynamic-update-slice_fusion.4
  151.9 5.7 bitcast_dynamic-update-slice_fusion.4
  213.7 5.7 bitcast_dynamic-update-slice_fusion.4
  227.3 250.6 %while.64 = (s32[]{:T(128)}, f32[4,8,2,8,512]{4,1,3,2,0:T(8,128)S(1)}, f32[8,2,8,512]{3,0,2,1:T(8,128)S(1)}, s32[]{:T(128)}, bf16[4,8,2,8,512]{4,1,3,2,0:T(8,128...) while((s32[]{:T(128)}, ...), condition=%wide.region_3.4_spmd, body=%wide.region_2.3_spmd.sunk | while | flops 67698688 | bytes 11829517 | solution.py:134
  241.4 9.3 %collective-permute-done.5 = f32[8,2,8,512]{3,0,2,1:T(8,128)S(1)} collective-permute-done((f32[8,2,8,512]{3,0,2,1:T(8,128)S(1)}, f32[8,2,8,512]{3,0,2,1:T(8,128)S(1)}, u32[]{:S(2)}, u32[]{:S(2)}) %collective-permute-start.5) | collective-permute-done | bytes 262176 | tf_op jit(solution)/shard_map/while/body/eval_jaxpr/ppermute | solution.py:27
  264.5 9.6 %collective-permute-done.5 = f32[8,2,8,512]{3,0,2,1:T(8,128)S(1)} collective-permute-done((f32[8,2,8,512]{3,0,2,1:T(8,128)S(1)}, f32[8,2,8,512]{3,0,2,1:T(8,128)S(1)}, u32[]{:S(2)}, u32[]{:S(2)}) %collective-permute-start.5) | collective-permute-done | bytes 262176 | tf_op jit(solution)/shard_map/while/body/eval_jaxpr/ppermute | solution.py:27
  287.6 9.4 %collective-permute-done.5 = f32[8,2,8,512]{3,0,2,1:T(8,128)S(1)} collective-permute-done((f32[8,2,8,512]{3,0,2,1:T(8,128)S(1)}, f32[8,2,8,512]{3,0,2,1:T(8,128)S(1)}, u32[]{:S(2)}, u32[]{:S(2)}) %collective-permute-start.5) | collective-permute-done | bytes 262176 | tf_op jit(solution)/shard_map/while/body/eval_jaxpr/ppermute | solution.py:27
  310.2 9.4 %collective-permute-done.5 = f32[8,2,8,512]{3,0,2,1:T(8,128)S(1)} collective-permute-done((f32[8,2,8,512]{3,0,2,1:T(8,128)S(1)}, f32[8,2,8,512]{3,0,2,1:T(8,128)S(1)}, u32[]{:S(2)}, u32[]{:S(2)}) %collective-permute-start.5) | collective-permute-done | bytes 262176 | tf_op jit(solution)/shard_map/while/body/eval_jaxpr/ppermute | solution.py:27
  332.8 9.4 %collective-permute-done.5 = f32[8,2,8,512]{3,0,2,1:T(8,128)S(1)} collective-permute-done((f32[8,2,8,512]{3,0,2,1:T(8,128)S(1)}, f32[8,2,8,512]{3,0,2,1:T(8,128)S(1)}, u32[]{:S(2)}, u32[]{:S(2)}) %collective-permute-start.5) | collective-permute-done | bytes 262176 | tf_op jit(solution)/shard_map/while/body/eval_jaxpr/ppermute | solution.py:27
  355.4 9.4 %collective-permute-done.5 = f32[8,2,8,512]{3,0,2,1:T(8,128)S(1)} collective-permute-done((f32[8,2,8,512]{3,0,2,1:T(8,128)S(1)}, f32[8,2,8,512]{3,0,2,1:T(8,128)S(1)}, u32[]{:S(2)}, u32[]{:S(2)}) %collective-permute-start.5) | collective-permute-done | bytes 262176 | tf_op jit(solution)/shard_map/while/body/eval_jaxpr/ppermute | solution.py:27
  378.1 9.4 %collective-permute-done.5 = f32[8,2,8,512]{3,0,2,1:T(8,128)S(1)} collective-permute-done((f32[8,2,8,512]{3,0,2,1:T(8,128)S(1)}, f32[8,2,8,512]{3,0,2,1:T(8,128)S(1)}, u32[]{:S(2)}, u32[]{:S(2)}) %collective-permute-start.5) | collective-permute-done | bytes 262176 | tf_op jit(solution)/shard_map/while/body/eval_jaxpr/ppermute | solution.py:27
  400.7 9.4 %collective-permute-done.5 = f32[8,2,8,512]{3,0,2,1:T(8,128)S(1)} collective-permute-done((f32[8,2,8,512]{3,0,2,1:T(8,128)S(1)}, f32[8,2,8,512]{3,0,2,1:T(8,128)S(1)}, u32[]{:S(2)}, u32[]{:S(2)}) %collective-permute-start.5) | collective-permute-done | bytes 262176 | tf_op jit(solution)/shard_map/while/body/eval_jaxpr/ppermute | solution.py:27
  423.3 9.4 %collective-permute-done.5 = f32[8,2,8,512]{3,0,2,1:T(8,128)S(1)} collective-permute-done((f32[8,2,8,512]{3,0,2,1:T(8,128)S(1)}, f32[8,2,8,512]{3,0,2,1:T(8,128)S(1)}, u32[]{:S(2)}, u32[]{:S(2)}) %collective-permute-start.5) | collective-permute-done | bytes 262176 | tf_op jit(solution)/shard_map/while/body/eval_jaxpr/ppermute | solution.py:27
  445.9 9.4 %collective-permute-done.5 = f32[8,2,8,512]{3,0,2,1:T(8,128)S(1)} collective-permute-done((f32[8,2,8,512]{3,0,2,1:T(8,128)S(1)}, f32[8,2,8,512]{3,0,2,1:T(8,128)S(1)}, u32[]{:S(2)}, u32[]{:S(2)}) %collective-permute-start.5) | collective-permute-done | bytes 262176 | tf_op jit(solution)/shard_map/while/body/eval_jaxpr/ppermute | solution.py:27
  468.6 9.4 %collective-permute-done.5 = f32[8,2,8,512]{3,0,2,1:T(8,128)S(1)} collective-permute-done((f32[8,2,8,512]{3,0,2,1:T(8,128)S(1)}, f32[8,2,8,512]{3,0,2,1:T(8,128)S(1)}, u32[]{:S(2)}, u32[]{:S(2)}) %collective-permute-start.5) | collective-permute-done | bytes 262176 | tf_op jit(solution)/shard_map/while/body/eval_jaxpr/ppermute | solution.py:27
  478.9 41.6 %psum.7 = f32[32,32]{1,0:T(8,128)S(1)} all-reduce(f32[32,32]{1,0:T(8,128)S(1)} %fusion.62), channel_id=1, replica_groups=mesh['layer'=8,'tile'=4] {'layer','tile'}, use_global_device_ids=true, to_apply=%region_4.5 | all-reduce | flops 1024 | bytes 8192 | tf_op jit(solution)/shard_map/psum | solution.py:143
  520.5 58.2 %while.66 = (s32[]{:T(128)}, f32[32,32]{1,0:T(8,128)S(1)}, f32[32,32]{1,0:T(8,128)S(1)}, s32[]{:T(128)}, s32[]{:T(128)}) while((s32[]{:T(128)}, f32[32,32]{1,0:T(8,128)S(1)}, f32[32,32]{1,0:T(8,128)S(1)}, s32[]{:T(128)}, s32[]{:T(128)}) %tuple.180), condition=%wide.region_7.8_spmd.clone.clone, body=%wide.region_5.7_spmd.clone.clone.sunk | while | flops 42338 | bytes 21869 | solution.py:43
  578.7 50.9 %while.65 = (s32[]{:T(128)}, f32[32,32]{1,0:T(8,128)S(1)}, f32[32,32]{1,0:T(8,128)S(1)}, s32[]{:T(128)}, s32[]{:T(128)}) while((s32[]{:T(128)}, f32[32,32]{1,0:T(8,128)S(1)}, f32[32,32]{1,0:T(8,128)S(1)}, s32[]{:T(128)}, s32[]{:T(128)}) %tuple.183), condition=%wide.region_10.11_spmd.clone, body=%wide.region_8.10_spmd.clone.sunk | while | flops 28994 | bytes 17244 | solution.py:57
  (576 shorter events, 419.4 us)
Async XLA Ops:
  17.0 5.9 collective-permute-start.2
  35.8 6.9 %collective-permute-start.2 = (bf16[8,2,8,512]{3,0,2,1:T(8,128)(2,1)S(1)}, bf16[8,2,8,512]{3,0,2,1:T(8,128)(2,1)S(1)}, u32[]{:S(2)}, u32[]{:S(2)}) collective-permute-start(bf16[8,2,8,512]{3,0,2,1:T(8,128)(2,1)S(1)} %bitcast.184), channel_id=1, source_target_pairs={{0,4},{4,8},{8,12},{12,16},{16,20},{20,24},{24,28},{1,5},{5,9},{9,... | collective-permute-start | bytes 393224 | tf_op jit(solution)/shard_map/while/body/eval_jaxpr/ppermute | solution.py:27
  42.7 5.6 collective-permute-start
  55.5 6.9 %collective-permute-start.2 = (bf16[8,2,8,512]{3,0,2,1:T(8,128)(2,1)S(1)}, bf16[8,2,8,512]{3,0,2,1:T(8,128)(2,1)S(1)}, u32[]{:S(2)}, u32[]{:S(2)}) collective-permute-start(bf16[8,2,8,512]{3,0,2,1:T(8,128)(2,1)S(1)} %bitcast.184), channel_id=1, source_target_pairs={{0,4},{4,8},{8,12},{12,16},{16,20},{20,24},{24,28},{1,5},{5,9},{9,... | collective-permute-start | bytes 393224 | tf_op jit(solution)/shard_map/while/body/eval_jaxpr/ppermute | solution.py:27
  75.2 7.8 %collective-permute-start.2 = (bf16[8,2,8,512]{3,0,2,1:T(8,128)(2,1)S(1)}, bf16[8,2,8,512]{3,0,2,1:T(8,128)(2,1)S(1)}, u32[]{:S(2)}, u32[]{:S(2)}) collective-permute-start(bf16[8,2,8,512]{3,0,2,1:T(8,128)(2,1)S(1)} %bitcast.184), channel_id=1, source_target_pairs={{0,4},{4,8},{8,12},{12,16},{16,20},{20,24},{24,28},{1,5},{5,9},{9,... | collective-permute-start | bytes 393224 | tf_op jit(solution)/shard_map/while/body/eval_jaxpr/ppermute | solution.py:27
  95.8 7.8 %collective-permute-start.2 = (bf16[8,2,8,512]{3,0,2,1:T(8,128)(2,1)S(1)}, bf16[8,2,8,512]{3,0,2,1:T(8,128)(2,1)S(1)}, u32[]{:S(2)}, u32[]{:S(2)}) collective-permute-start(bf16[8,2,8,512]{3,0,2,1:T(8,128)(2,1)S(1)} %bitcast.184), channel_id=1, source_target_pairs={{0,4},{4,8},{8,12},{12,16},{16,20},{20,24},{24,28},{1,5},{5,9},{9,... | collective-permute-start | bytes 393224 | tf_op jit(solution)/shard_map/while/body/eval_jaxpr/ppermute | solution.py:27
  103.6 5.6 collective-permute-start
  116.4 7.8 %collective-permute-start.2 = (bf16[8,2,8,512]{3,0,2,1:T(8,128)(2,1)S(1)}, bf16[8,2,8,512]{3,0,2,1:T(8,128)(2,1)S(1)}, u32[]{:S(2)}, u32[]{:S(2)}) collective-permute-start(bf16[8,2,8,512]{3,0,2,1:T(8,128)(2,1)S(1)} %bitcast.184), channel_id=1, source_target_pairs={{0,4},{4,8},{8,12},{12,16},{16,20},{20,24},{24,28},{1,5},{5,9},{9,... | collective-permute-start | bytes 393224 | tf_op jit(solution)/shard_map/while/body/eval_jaxpr/ppermute | solution.py:27
  137.0 7.8 %collective-permute-start.2 = (bf16[8,2,8,512]{3,0,2,1:T(8,128)(2,1)S(1)}, bf16[8,2,8,512]{3,0,2,1:T(8,128)(2,1)S(1)}, u32[]{:S(2)}, u32[]{:S(2)}) collective-permute-start(bf16[8,2,8,512]{3,0,2,1:T(8,128)(2,1)S(1)} %bitcast.184), channel_id=1, source_target_pairs={{0,4},{4,8},{8,12},{12,16},{16,20},{20,24},{24,28},{1,5},{5,9},{9,... | collective-permute-start | bytes 393224 | tf_op jit(solution)/shard_map/while/body/eval_jaxpr/ppermute | solution.py:27
  157.6 7.8 %collective-permute-start.2 = (bf16[8,2,8,512]{3,0,2,1:T(8,128)(2,1)S(1)}, bf16[8,2,8,512]{3,0,2,1:T(8,128)(2,1)S(1)}, u32[]{:S(2)}, u32[]{:S(2)}) collective-permute-start(bf16[8,2,8,512]{3,0,2,1:T(8,128)(2,1)S(1)} %bitcast.184), channel_id=1, source_target_pairs={{0,4},{4,8},{8,12},{12,16},{16,20},{20,24},{24,28},{1,5},{5,9},{9,... | collective-permute-start | bytes 393224 | tf_op jit(solution)/shard_map/while/body/eval_jaxpr/ppermute | solution.py:27
  178.2 7.8 %collective-permute-start.2 = (bf16[8,2,8,512]{3,0,2,1:T(8,128)(2,1)S(1)}, bf16[8,2,8,512]{3,0,2,1:T(8,128)(2,1)S(1)}, u32[]{:S(2)}, u32[]{:S(2)}) collective-permute-start(bf16[8,2,8,512]{3,0,2,1:T(8,128)(2,1)S(1)} %bitcast.184), channel_id=1, source_target_pairs={{0,4},{4,8},{8,12},{12,16},{16,20},{20,24},{24,28},{1,5},{5,9},{9,... | collective-permute-start | bytes 393224 | tf_op jit(solution)/shard_map/while/body/eval_jaxpr/ppermute | solution.py:27
  198.8 7.8 %collective-permute-start.2 = (bf16[8,2,8,512]{3,0,2,1:T(8,128)(2,1)S(1)}, bf16[8,2,8,512]{3,0,2,1:T(8,128)(2,1)S(1)}, u32[]{:S(2)}, u32[]{:S(2)}) collective-permute-start(bf16[8,2,8,512]{3,0,2,1:T(8,128)(2,1)S(1)} %bitcast.184), channel_id=1, source_target_pairs={{0,4},{4,8},{8,12},{12,16},{16,20},{20,24},{24,28},{1,5},{5,9},{9,... | collective-permute-start | bytes 393224 | tf_op jit(solution)/shard_map/while/body/eval_jaxpr/ppermute | solution.py:27
  219.4 7.8 %collective-permute-start.2 = (bf16[8,2,8,512]{3,0,2,1:T(8,128)(2,1)S(1)}, bf16[8,2,8,512]{3,0,2,1:T(8,128)(2,1)S(1)}, u32[]{:S(2)}, u32[]{:S(2)}) collective-permute-start(bf16[8,2,8,512]{3,0,2,1:T(8,128)(2,1)S(1)} %bitcast.184), channel_id=1, source_target_pairs={{0,4},{4,8},{8,12},{12,16},{16,20},{20,24},{24,28},{1,5},{5,9},{9,... | collective-permute-start | bytes 393224 | tf_op jit(solution)/shard_map/while/body/eval_jaxpr/ppermute | solution.py:27
  240.1 10.6 %collective-permute-start.5 = (f32[8,2,8,512]{3,0,2,1:T(8,128)S(1)}, f32[8,2,8,512]{3,0,2,1:T(8,128)S(1)}, u32[]{:S(2)}, u32[]{:S(2)}) collective-permute-start(f32[8,2,8,512]{3,0,2,1:T(8,128)S(1)} %get-tuple-element.874), channel_id=1, source_target_pairs={{4,0},{8,4},{12,8},{16,12},{20,16},{24,20},{28,24},{5,1},{9,5},{13... | collective-permute-start | bytes 786440 | tf_op jit(solution)/shard_map/while/body/eval_jaxpr/ppermute | solution.py:27
  263.2 11.0 %collective-permute-start.5 = (f32[8,2,8,512]{3,0,2,1:T(8,128)S(1)}, f32[8,2,8,512]{3,0,2,1:T(8,128)S(1)}, u32[]{:S(2)}, u32[]{:S(2)}) collective-permute-start(f32[8,2,8,512]{3,0,2,1:T(8,128)S(1)} %get-tuple-element.874), channel_id=1, source_target_pairs={{4,0},{8,4},{12,8},{16,12},{20,16},{24,20},{28,24},{5,1},{9,5},{13... | collective-permute-start | bytes 786440 | tf_op jit(solution)/shard_map/while/body/eval_jaxpr/ppermute | solution.py:27
  286.3 10.7 %collective-permute-start.5 = (f32[8,2,8,512]{3,0,2,1:T(8,128)S(1)}, f32[8,2,8,512]{3,0,2,1:T(8,128)S(1)}, u32[]{:S(2)}, u32[]{:S(2)}) collective-permute-start(f32[8,2,8,512]{3,0,2,1:T(8,128)S(1)} %get-tuple-element.874), channel_id=1, source_target_pairs={{4,0},{8,4},{12,8},{16,12},{20,16},{24,20},{28,24},{5,1},{9,5},{13... | collective-permute-start | bytes 786440 | tf_op jit(solution)/shard_map/while/body/eval_jaxpr/ppermute | solution.py:27
  308.9 10.7 %collective-permute-start.5 = (f32[8,2,8,512]{3,0,2,1:T(8,128)S(1)}, f32[8,2,8,512]{3,0,2,1:T(8,128)S(1)}, u32[]{:S(2)}, u32[]{:S(2)}) collective-permute-start(f32[8,2,8,512]{3,0,2,1:T(8,128)S(1)} %get-tuple-element.874), channel_id=1, source_target_pairs={{4,0},{8,4},{12,8},{16,12},{20,16},{24,20},{28,24},{5,1},{9,5},{13... | collective-permute-start | bytes 786440 | tf_op jit(solution)/shard_map/while/body/eval_jaxpr/ppermute | solution.py:27
  331.5 10.7 %collective-permute-start.5 = (f32[8,2,8,512]{3,0,2,1:T(8,128)S(1)}, f32[8,2,8,512]{3,0,2,1:T(8,128)S(1)}, u32[]{:S(2)}, u32[]{:S(2)}) collective-permute-start(f32[8,2,8,512]{3,0,2,1:T(8,128)S(1)} %get-tuple-element.874), channel_id=1, source_target_pairs={{4,0},{8,4},{12,8},{16,12},{20,16},{24,20},{28,24},{5,1},{9,5},{13... | collective-permute-start | bytes 786440 | tf_op jit(solution)/shard_map/while/body/eval_jaxpr/ppermute | solution.py:27
  354.1 10.7 %collective-permute-start.5 = (f32[8,2,8,512]{3,0,2,1:T(8,128)S(1)}, f32[8,2,8,512]{3,0,2,1:T(8,128)S(1)}, u32[]{:S(2)}, u32[]{:S(2)}) collective-permute-start(f32[8,2,8,512]{3,0,2,1:T(8,128)S(1)} %get-tuple-element.874), channel_id=1, source_target_pairs={{4,0},{8,4},{12,8},{16,12},{20,16},{24,20},{28,24},{5,1},{9,5},{13... | collective-permute-start | bytes 786440 | tf_op jit(solution)/shard_map/while/body/eval_jaxpr/ppermute | solution.py:27
  376.8 10.7 %collective-permute-start.5 = (f32[8,2,8,512]{3,0,2,1:T(8,128)S(1)}, f32[8,2,8,512]{3,0,2,1:T(8,128)S(1)}, u32[]{:S(2)}, u32[]{:S(2)}) collective-permute-start(f32[8,2,8,512]{3,0,2,1:T(8,128)S(1)} %get-tuple-element.874), channel_id=1, source_target_pairs={{4,0},{8,4},{12,8},{16,12},{20,16},{24,20},{28,24},{5,1},{9,5},{13... | collective-permute-start | bytes 786440 | tf_op jit(solution)/shard_map/while/body/eval_jaxpr/ppermute | solution.py:27
  399.4 10.7 %collective-permute-start.5 = (f32[8,2,8,512]{3,0,2,1:T(8,128)S(1)}, f32[8,2,8,512]{3,0,2,1:T(8,128)S(1)}, u32[]{:S(2)}, u32[]{:S(2)}) collective-permute-start(f32[8,2,8,512]{3,0,2,1:T(8,128)S(1)} %get-tuple-element.874), channel_id=1, source_target_pairs={{4,0},{8,4},{12,8},{16,12},{20,16},{24,20},{28,24},{5,1},{9,5},{13... | collective-permute-start | bytes 786440 | tf_op jit(solution)/shard_map/while/body/eval_jaxpr/ppermute | solution.py:27
  422.0 10.7 %collective-permute-start.5 = (f32[8,2,8,512]{3,0,2,1:T(8,128)S(1)}, f32[8,2,8,512]{3,0,2,1:T(8,128)S(1)}, u32[]{:S(2)}, u32[]{:S(2)}) collective-permute-start(f32[8,2,8,512]{3,0,2,1:T(8,128)S(1)} %get-tuple-element.874), channel_id=1, source_target_pairs={{4,0},{8,4},{12,8},{16,12},{20,16},{24,20},{28,24},{5,1},{9,5},{13... | collective-permute-start | bytes 786440 | tf_op jit(solution)/shard_map/while/body/eval_jaxpr/ppermute | solution.py:27
  444.6 10.7 %collective-permute-start.5 = (f32[8,2,8,512]{3,0,2,1:T(8,128)S(1)}, f32[8,2,8,512]{3,0,2,1:T(8,128)S(1)}, u32[]{:S(2)}, u32[]{:S(2)}) collective-permute-start(f32[8,2,8,512]{3,0,2,1:T(8,128)S(1)} %get-tuple-element.874), channel_id=1, source_target_pairs={{4,0},{8,4},{12,8},{16,12},{20,16},{24,20},{28,24},{5,1},{9,5},{13... | collective-permute-start | bytes 786440 | tf_op jit(solution)/shard_map/while/body/eval_jaxpr/ppermute | solution.py:27
  467.3 10.7 %collective-permute-start.5 = (f32[8,2,8,512]{3,0,2,1:T(8,128)S(1)}, f32[8,2,8,512]{3,0,2,1:T(8,128)S(1)}, u32[]{:S(2)}, u32[]{:S(2)}) collective-permute-start(f32[8,2,8,512]{3,0,2,1:T(8,128)S(1)} %get-tuple-element.874), channel_id=1, source_target_pairs={{4,0},{8,4},{12,8},{16,12},{20,16},{24,20},{28,24},{5,1},{9,5},{13... | collective-permute-start | bytes 786440 | tf_op jit(solution)/shard_map/while/body/eval_jaxpr/ppermute | solution.py:27
  (42 other events, 181.2 us)
where the time goes:
time: 640 us; the launch traced here: 634 us
  matrix products  208 us (32%)
  starting transfers between devices  169 us (26%)
  waiting for transfers between devices  159 us (25%)
  blocking collectives  41.6 us (6%)
  loops' own time  24 us (4%)
  local copies, waits for them, and re-layouts  21 us (3%)
  other arithmetic  11.1 us (2%)
    ppermute x22, waiting for transfers between devices, shifted(): return lax.ppermute(array, axis, pairs)  131 us
    dot_general x22, matrix products, apply_inverse(): jnp.einsum('crik,jcrk->jcri', inverse_block, vectors, preferred_element_t...  124 us
    ppermute x22, starting transfers between devices, with_halo(): lax.ppermute(tail, axis, [(i, (i + 1) % count) for i in range(ends)])  72.2 us
    ppermute x22, starting transfers between devices, shifted(): return lax.ppermute(array, axis, pairs)  68.5 us
    psum x1, blocking collectives, per_device(): gram_whole = lax.psum(gram_local, ('layer', 'tile'))  41.6 us
    ppermute x22, starting transfers between devices, with_halo(): lax.ppermute(head, axis, [((i + 1) % count, i) for i in range(ends)])  28.4 us
    ppermute x22, waiting for transfers between devices, with_halo(): lax.ppermute(head, axis, [((i + 1) % count, i) for i in range(ends)])  27.9 us
    dot_general x32, matrix products, column_step(): column = column - jnp.dot(lower, lower_row, precision=lax.Precision.HIGHEST)  24.9 us
  transfers between devices with their start and end apart: 66, of which 44 were waited for; matrix products, arithmetic and copies ran while one was open for 3% of the time, Pallas kernels for 0%

commit v1 on v0

--- a/solution.py
+++ b/solution.py
@@ -140,7 +140,7 @@
     columns_mat = up_store.reshape(column_total, -1)
     gram_local = jnp.dot(columns_mat, columns_mat.T, precision=lax.Precision.HIGHEST)
     total_rows = layers_total * tile_count * columns_mat.shape[1]
-    gram_whole = lax.psum(gram_local, ("layer", "tile"))
+    gram_whole = lax.psum(lax.psum(gram_local, "tile"), "layer")
     triangle = lower_factor(gram_whole / total_rows).T
     solved = jnp.dot(lower_inverse(triangle.T), columns_mat, precision=lax.Precision.HIGHEST)
     basis_out = solved.reshape(1, column_total, 2, rows_dev, plane_width)

time: 640 us -> 645 us (level)
    psum x1 -> x2, blocking collectives: 41.6 us -> 47.1 us  [per_device(): gram_whole = lax.psum(lax.psum(gram_local, 'tile'), 'layer')]
where the time goes in v1:
time: 645 us; the launch traced here: 640 us
  matrix products  208 us (32%)
  starting transfers between devices  169 us (26%)
  waiting for transfers between devices  159 us (25%)
  blocking collectives  47.1 us (7%)
  loops' own time  24 us (4%)
  local copies, waits for them, and re-layouts  21 us (3%)
  other arithmetic  11.2 us (2%)
    ppermute x22, waiting for transfers between devices, shifted(): return lax.ppermute(array, axis, pairs)  131 us
    dot_general x22, matrix products, apply_inverse(): jnp.einsum('crik,jcrk->jcri', inverse_block, vectors, preferred_element_t...  124 us
    ppermute x22, starting transfers between devices, with_halo(): lax.ppermute(tail, axis, [(i, (i + 1) % count) for i in range(ends)])  72.2 us
    ppermute x22, starting transfers between devices, shifted(): return lax.ppermute(array, axis, pairs)  68.5 us
    psum x2, blocking collectives, per_device(): gram_whole = lax.psum(lax.psum(gram_local, 'tile'), 'layer')  47.1 us
    ppermute x22, starting transfers between devices, with_halo(): lax.ppermute(head, axis, [((i + 1) % count, i) for i in range(ends)])  28.4 us
    ppermute x22, waiting for transfers between devices, with_halo(): lax.ppermute(head, axis, [((i + 1) % count, i) for i in range(ends)])  27.9 us
    dot_general x32, matrix products, column_step(): column = column - jnp.dot(lower, lower_row, precision=lax.Precision.HIGHEST)  24.9 us
  transfers between devices with their start and end apart: 66, of which 44 were waited for; matrix products, arithmetic and copies ran while one was open for 3% of the time, Pallas kernels for 0%

profile of v1, /device:TPU:0, one launch (start us, length us, event | category | flops | bytes accessed | tf_op | source)
XLA Modules:
  0.0 639.6 jit_solution(15160661912539070682)
XLA Ops:
  3.6 223.6 %while.63 = (s32[]{:T(128)}, bf16[4,8,2,8,512]{4,1,3,2,0:T(8,128)(2,1)S(1)}, bf16[8,2,8,512]{3,0,2,1:T(8,128)(2,1)S(1)}, s32[]{:T(128)}, f32[4,8,2,8,512]{4,3,2,...) while((s32[]{:T(128)}, ...), condition=%wide.region_1.2_spmd, body=%wide.region_0.1_spmd.sunk | while | flops 67829760 | bytes 11698449 | solution.py:116
  11.4 5.7 bitcast_dynamic-update-slice_fusion.4
  30.1 5.7 bitcast_dynamic-update-slice_fusion.4
  69.5 5.7 bitcast_dynamic-update-slice_fusion.4
  90.1 5.7 bitcast_dynamic-update-slice_fusion.4
  131.3 5.7 bitcast_dynamic-update-slice_fusion.4
  151.9 5.7 bitcast_dynamic-update-slice_fusion.4
  213.7 5.7 bitcast_dynamic-update-slice_fusion.4
  227.3 250.6 %while.64 = (s32[]{:T(128)}, f32[4,8,2,8,512]{4,1,3,2,0:T(8,128)S(1)}, f32[8,2,8,512]{3,0,2,1:T(8,128)S(1)}, s32[]{:T(128)}, bf16[4,8,2,8,512]{4,1,3,2,0:T(8,128...) while((s32[]{:T(128)}, ...), condition=%wide.region_3.4_spmd, body=%wide.region_2.3_spmd.sunk | while | flops 67698688 | bytes 11829517 | solution.py:134
  241.4 9.3 %collective-permute-done.5 = f32[8,2,8,512]{3,0,2,1:T(8,128)S(1)} collective-permute-done((f32[8,2,8,512]{3,0,2,1:T(8,128)S(1)}, f32[8,2,8,512]{3,0,2,1:T(8,128)S(1)}, u32[]{:S(2)}, u32[]{:S(2)}) %collective-permute-start.5) | collective-permute-done | bytes 262176 | tf_op jit(solution)/shard_map/while/body/eval_jaxpr/ppermute | solution.py:27
  264.5 9.6 %collective-permute-done.5 = f32[8,2,8,512]{3,0,2,1:T(8,128)S(1)} collective-permute-done((f32[8,2,8,512]{3,0,2,1:T(8,128)S(1)}, f32[8,2,8,512]{3,0,2,1:T(8,128)S(1)}, u32[]{:S(2)}, u32[]{:S(2)}) %collective-permute-start.5) | collective-permute-done | bytes 262176 | tf_op jit(solution)/shard_map/while/body/eval_jaxpr/ppermute | solution.py:27
  287.6 9.4 %collective-permute-done.5 = f32[8,2,8,512]{3,0,2,1:T(8,128)S(1)} collective-permute-done((f32[8,2,8,512]{3,0,2,1:T(8,128)S(1)}, f32[8,2,8,512]{3,0,2,1:T(8,128)S(1)}, u32[]{:S(2)}, u32[]{:S(2)}) %collective-permute-start.5) | collective-permute-done | bytes 262176 | tf_op jit(solution)/shard_map/while/body/eval_jaxpr/ppermute | solution.py:27
  310.2 9.4 %collective-permute-done.5 = f32[8,2,8,512]{3,0,2,1:T(8,128)S(1)} collective-permute-done((f32[8,2,8,512]{3,0,2,1:T(8,128)S(1)}, f32[8,2,8,512]{3,0,2,1:T(8,128)S(1)}, u32[]{:S(2)}, u32[]{:S(2)}) %collective-permute-start.5) | collective-permute-done | bytes 262176 | tf_op jit(solution)/shard_map/while/body/eval_jaxpr/ppermute | solution.py:27
  332.8 9.4 %collective-permute-done.5 = f32[8,2,8,512]{3,0,2,1:T(8,128)S(1)} collective-permute-done((f32[8,2,8,512]{3,0,2,1:T(8,128)S(1)}, f32[8,2,8,512]{3,0,2,1:T(8,128)S(1)}, u32[]{:S(2)}, u32[]{:S(2)}) %collective-permute-start.5) | collective-permute-done | bytes 262176 | tf_op jit(solution)/shard_map/while/body/eval_jaxpr/ppermute | solution.py:27
  355.4 9.4 %collective-permute-done.5 = f32[8,2,8,512]{3,0,2,1:T(8,128)S(1)} collective-permute-done((f32[8,2,8,512]{3,0,2,1:T(8,128)S(1)}, f32[8,2,8,512]{3,0,2,1:T(8,128)S(1)}, u32[]{:S(2)}, u32[]{:S(2)}) %collective-permute-start.5) | collective-permute-done | bytes 262176 | tf_op jit(solution)/shard_map/while/body/eval_jaxpr/ppermute | solution.py:27
  378.1 9.4 %collective-permute-done.5 = f32[8,2,8,512]{3,0,2,1:T(8,128)S(1)} collective-permute-done((f32[8,2,8,512]{3,0,2,1:T(8,128)S(1)}, f32[8,2,8,512]{3,0,2,1:T(8,128)S(1)}, u32[]{:S(2)}, u32[]{:S(2)}) %collective-permute-start.5) | collective-permute-done | bytes 262176 | tf_op jit(solution)/shard_map/while/body/eval_jaxpr/ppermute | solution.py:27
  400.7 9.4 %collective-permute-done.5 = f32[8,2,8,512]{3,0,2,1:T(8,128)S(1)} collective-permute-done((f32[8,2,8,512]{3,0,2,1:T(8,128)S(1)}, f32[8,2,8,512]{3,0,2,1:T(8,128)S(1)}, u32[]{:S(2)}, u32[]{:S(2)}) %collective-permute-start.5) | collective-permute-done | bytes 262176 | tf_op jit(solution)/shard_map/while/body/eval_jaxpr/ppermute | solution.py:27
  423.3 9.4 %collective-permute-done.5 = f32[8,2,8,512]{3,0,2,1:T(8,128)S(1)} collective-permute-done((f32[8,2,8,512]{3,0,2,1:T(8,128)S(1)}, f32[8,2,8,512]{3,0,2,1:T(8,128)S(1)}, u32[]{:S(2)}, u32[]{:S(2)}) %collective-permute-start.5) | collective-permute-done | bytes 262176 | tf_op jit(solution)/shard_map/while/body/eval_jaxpr/ppermute | solution.py:27
  445.9 9.4 %collective-permute-done.5 = f32[8,2,8,512]{3,0,2,1:T(8,128)S(1)} collective-permute-done((f32[8,2,8,512]{3,0,2,1:T(8,128)S(1)}, f32[8,2,8,512]{3,0,2,1:T(8,128)S(1)}, u32[]{:S(2)}, u32[]{:S(2)}) %collective-permute-start.5) | collective-permute-done | bytes 262176 | tf_op jit(solution)/shard_map/while/body/eval_jaxpr/ppermute | solution.py:27
  468.6 9.4 %collective-permute-done.5 = f32[8,2,8,512]{3,0,2,1:T(8,128)S(1)} collective-permute-done((f32[8,2,8,512]{3,0,2,1:T(8,128)S(1)}, f32[8,2,8,512]{3,0,2,1:T(8,128)S(1)}, u32[]{:S(2)}, u32[]{:S(2)}) %collective-permute-start.5) | collective-permute-done | bytes 262176 | tf_op jit(solution)/shard_map/while/body/eval_jaxpr/ppermute | solution.py:27
  478.9 11.1 %psum.14 = f32[32,32]{1,0:T(8,128)S(1)} all-reduce(f32[32,32]{1,0:T(8,128)S(1)} %fusion.62), channel_id=1, replica_groups=mesh['layer'=8,'tile'=4] {'tile'}, use_global_device_ids=true, to_apply=%region_4.5 | all-reduce | flops 1024 | bytes 8192 | tf_op jit(solution)/shard_map/psum | solution.py:143
  490.0 36.0 %psum.15 = f32[32,32]{1,0:T(8,128)S(1)} all-reduce(f32[32,32]{1,0:T(8,128)S(1)} %psum.14), channel_id=1, replica_groups=mesh['layer'=8,'tile'=4] {'layer'}, use_global_device_ids=true, to_apply=%region_5.6 | all-reduce | flops 1024 | bytes 8192 | tf_op jit(solution)/shard_map/psum | solution.py:143
  526.0 58.2 %while.66 = (s32[]{:T(128)}, f32[32,32]{1,0:T(8,128)S(1)}, f32[32,32]{1,0:T(8,128)S(1)}, s32[]{:T(128)}, s32[]{:T(128)}) while((s32[]{:T(128)}, f32[32,32]{1,0:T(8,128)S(1)}, f32[32,32]{1,0:T(8,128)S(1)}, s32[]{:T(128)}, s32[]{:T(128)}) %tuple.180), condition=%wide.region_8.9_spmd.clone.clone, body=%wide.region_6.8_spmd.clone.clone.sunk | while | flops 42338 | bytes 21869 | solution.py:43
  584.2 50.9 %while.65 = (s32[]{:T(128)}, f32[32,32]{1,0:T(8,128)S(1)}, f32[32,32]{1,0:T(8,128)S(1)}, s32[]{:T(128)}, s32[]{:T(128)}) while((s32[]{:T(128)}, f32[32,32]{1,0:T(8,128)S(1)}, f32[32,32]{1,0:T(8,128)S(1)}, s32[]{:T(128)}, s32[]{:T(128)}) %tuple.183), condition=%wide.region_11.12_spmd.clone, body=%wide.region_9.11_spmd.clone.sunk | while | flops 28994 | bytes 17244 | solution.py:57
  (577 shorter events, 425.1 us)
Async XLA Ops:
  17.0 5.9 collective-permute-start.2
  35.8 6.9 %collective-permute-start.2 = (bf16[8,2,8,512]{3,0,2,1:T(8,128)(2,1)S(1)}, bf16[8,2,8,512]{3,0,2,1:T(8,128)(2,1)S(1)}, u32[]{:S(2)}, u32[]{:S(2)}) collective-permute-start(bf16[8,2,8,512]{3,0,2,1:T(8,128)(2,1)S(1)} %bitcast.184), channel_id=1, source_target_pairs={{0,4},{4,8},{8,12},{12,16},{16,20},{20,24},{24,28},{1,5},{5,9},{9,... | collective-permute-start | bytes 393224 | tf_op jit(solution)/shard_map/while/body/eval_jaxpr/ppermute | solution.py:27
  42.7 5.6 collective-permute-start
  55.5 6.9 %collective-permute-start.2 = (bf16[8,2,8,512]{3,0,2,1:T(8,128)(2,1)S(1)}, bf16[8,2,8,512]{3,0,2,1:T(8,128)(2,1)S(1)}, u32[]{:S(2)}, u32[]{:S(2)}) collective-permute-start(bf16[8,2,8,512]{3,0,2,1:T(8,128)(2,1)S(1)} %bitcast.184), channel_id=1, source_target_pairs={{0,4},{4,8},{8,12},{12,16},{16,20},{20,24},{24,28},{1,5},{5,9},{9,... | collective-permute-start | bytes 393224 | tf_op jit(solution)/shard_map/while/body/eval_jaxpr/ppermute | solution.py:27
  75.2 7.8 %collective-permute-start.2 = (bf16[8,2,8,512]{3,0,2,1:T(8,128)(2,1)S(1)}, bf16[8,2,8,512]{3,0,2,1:T(8,128)(2,1)S(1)}, u32[]{:S(2)}, u32[]{:S(2)}) collective-permute-start(bf16[8,2,8,512]{3,0,2,1:T(8,128)(2,1)S(1)} %bitcast.184), channel_id=1, source_target_pairs={{0,4},{4,8},{8,12},{12,16},{16,20},{20,24},{24,28},{1,5},{5,9},{9,... | collective-permute-start | bytes 393224 | tf_op jit(solution)/shard_map/while/body/eval_jaxpr/ppermute | solution.py:27
  95.8 7.8 %collective-permute-start.2 = (bf16[8,2,8,512]{3,0,2,1:T(8,128)(2,1)S(1)}, bf16[8,2,8,512]{3,0,2,1:T(8,128)(2,1)S(1)}, u32[]{:S(2)}, u32[]{:S(2)}) collective-permute-start(bf16[8,2,8,512]{3,0,2,1:T(8,128)(2,1)S(1)} %bitcast.184), channel_id=1, source_target_pairs={{0,4},{4,8},{8,12},{12,16},{16,20},{20,24},{24,28},{1,5},{5,9},{9,... | collective-permute-start | bytes 393224 | tf_op jit(solution)/shard_map/while/body/eval_jaxpr/ppermute | solution.py:27
  103.6 5.6 collective-permute-start
  116.4 7.8 %collective-permute-start.2 = (bf16[8,2,8,512]{3,0,2,1:T(8,128)(2,1)S(1)}, bf16[8,2,8,512]{3,0,2,1:T(8,128)(2,1)S(1)}, u32[]{:S(2)}, u32[]{:S(2)}) collective-permute-start(bf16[8,2,8,512]{3,0,2,1:T(8,128)(2,1)S(1)} %bitcast.184), channel_id=1, source_target_pairs={{0,4},{4,8},{8,12},{12,16},{16,20},{20,24},{24,28},{1,5},{5,9},{9,... | collective-permute-start | bytes 393224 | tf_op jit(solution)/shard_map/while/body/eval_jaxpr/ppermute | solution.py:27
  137.0 7.8 %collective-permute-start.2 = (bf16[8,2,8,512]{3,0,2,1:T(8,128)(2,1)S(1)}, bf16[8,2,8,512]{3,0,2,1:T(8,128)(2,1)S(1)}, u32[]{:S(2)}, u32[]{:S(2)}) collective-permute-start(bf16[8,2,8,512]{3,0,2,1:T(8,128)(2,1)S(1)} %bitcast.184), channel_id=1, source_target_pairs={{0,4},{4,8},{8,12},{12,16},{16,20},{20,24},{24,28},{1,5},{5,9},{9,... | collective-permute-start | bytes 393224 | tf_op jit(solution)/shard_map/while/body/eval_jaxpr/ppermute | solution.py:27
  157.6 7.8 %collective-permute-start.2 = (bf16[8,2,8,512]{3,0,2,1:T(8,128)(2,1)S(1)}, bf16[8,2,8,512]{3,0,2,1:T(8,128)(2,1)S(1)}, u32[]{:S(2)}, u32[]{:S(2)}) collective-permute-start(bf16[8,2,8,512]{3,0,2,1:T(8,128)(2,1)S(1)} %bitcast.184), channel_id=1, source_target_pairs={{0,4},{4,8},{8,12},{12,16},{16,20},{20,24},{24,28},{1,5},{5,9},{9,... | collective-permute-start | bytes 393224 | tf_op jit(solution)/shard_map/while/body/eval_jaxpr/ppermute | solution.py:27
  178.2 7.8 %collective-permute-start.2 = (bf16[8,2,8,512]{3,0,2,1:T(8,128)(2,1)S(1)}, bf16[8,2,8,512]{3,0,2,1:T(8,128)(2,1)S(1)}, u32[]{:S(2)}, u32[]{:S(2)}) collective-permute-start(bf16[8,2,8,512]{3,0,2,1:T(8,128)(2,1)S(1)} %bitcast.184), channel_id=1, source_target_pairs={{0,4},{4,8},{8,12},{12,16},{16,20},{20,24},{24,28},{1,5},{5,9},{9,... | collective-permute-start | bytes 393224 | tf_op jit(solution)/shard_map/while/body/eval_jaxpr/ppermute | solution.py:27
  198.8 7.8 %collective-permute-start.2 = (bf16[8,2,8,512]{3,0,2,1:T(8,128)(2,1)S(1)}, bf16[8,2,8,512]{3,0,2,1:T(8,128)(2,1)S(1)}, u32[]{:S(2)}, u32[]{:S(2)}) collective-permute-start(bf16[8,2,8,512]{3,0,2,1:T(8,128)(2,1)S(1)} %bitcast.184), channel_id=1, source_target_pairs={{0,4},{4,8},{8,12},{12,16},{16,20},{20,24},{24,28},{1,5},{5,9},{9,... | collective-permute-start | bytes 393224 | tf_op jit(solution)/shard_map/while/body/eval_jaxpr/ppermute | solution.py:27
  219.4 7.8 %collective-permute-start.2 = (bf16[8,2,8,512]{3,0,2,1:T(8,128)(2,1)S(1)}, bf16[8,2,8,512]{3,0,2,1:T(8,128)(2,1)S(1)}, u32[]{:S(2)}, u32[]{:S(2)}) collective-permute-start(bf16[8,2,8,512]{3,0,2,1:T(8,128)(2,1)S(1)} %bitcast.184), channel_id=1, source_target_pairs={{0,4},{4,8},{8,12},{12,16},{16,20},{20,24},{24,28},{1,5},{5,9},{9,... | collective-permute-start | bytes 393224 | tf_op jit(solution)/shard_map/while/body/eval_jaxpr/ppermute | solution.py:27
  240.1 10.6 %collective-permute-start.5 = (f32[8,2,8,512]{3,0,2,1:T(8,128)S(1)}, f32[8,2,8,512]{3,0,2,1:T(8,128)S(1)}, u32[]{:S(2)}, u32[]{:S(2)}) collective-permute-start(f32[8,2,8,512]{3,0,2,1:T(8,128)S(1)} %get-tuple-element.874), channel_id=1, source_target_pairs={{4,0},{8,4},{12,8},{16,12},{20,16},{24,20},{28,24},{5,1},{9,5},{13... | collective-permute-start | bytes 786440 | tf_op jit(solution)/shard_map/while/body/eval_jaxpr/ppermute | solution.py:27
  263.2 11.0 %collective-permute-start.5 = (f32[8,2,8,512]{3,0,2,1:T(8,128)S(1)}, f32[8,2,8,512]{3,0,2,1:T(8,128)S(1)}, u32[]{:S(2)}, u32[]{:S(2)}) collective-permute-start(f32[8,2,8,512]{3,0,2,1:T(8,128)S(1)} %get-tuple-element.874), channel_id=1, source_target_pairs={{4,0},{8,4},{12,8},{16,12},{20,16},{24,20},{28,24},{5,1},{9,5},{13... | collective-permute-start | bytes 786440 | tf_op jit(solution)/shard_map/while/body/eval_jaxpr/ppermute | solution.py:27
  286.3 10.7 %collective-permute-start.5 = (f32[8,2,8,512]{3,0,2,1:T(8,128)S(1)}, f32[8,2,8,512]{3,0,2,1:T(8,128)S(1)}, u32[]{:S(2)}, u32[]{:S(2)}) collective-permute-start(f32[8,2,8,512]{3,0,2,1:T(8,128)S(1)} %get-tuple-element.874), channel_id=1, source_target_pairs={{4,0},{8,4},{12,8},{16,12},{20,16},{24,20},{28,24},{5,1},{9,5},{13... | collective-permute-start | bytes 786440 | tf_op jit(solution)/shard_map/while/body/eval_jaxpr/ppermute | solution.py:27
  308.9 10.7 %collective-permute-start.5 = (f32[8,2,8,512]{3,0,2,1:T(8,128)S(1)}, f32[8,2,8,512]{3,0,2,1:T(8,128)S(1)}, u32[]{:S(2)}, u32[]{:S(2)}) collective-permute-start(f32[8,2,8,512]{3,0,2,1:T(8,128)S(1)} %get-tuple-element.874), channel_id=1, source_target_pairs={{4,0},{8,4},{12,8},{16,12},{20,16},{24,20},{28,24},{5,1},{9,5},{13... | collective-permute-start | bytes 786440 | tf_op jit(solution)/shard_map/while/body/eval_jaxpr/ppermute | solution.py:27
  331.5 10.7 %collective-permute-start.5 = (f32[8,2,8,512]{3,0,2,1:T(8,128)S(1)}, f32[8,2,8,512]{3,0,2,1:T(8,128)S(1)}, u32[]{:S(2)}, u32[]{:S(2)}) collective-permute-start(f32[8,2,8,512]{3,0,2,1:T(8,128)S(1)} %get-tuple-element.874), channel_id=1, source_target_pairs={{4,0},{8,4},{12,8},{16,12},{20,16},{24,20},{28,24},{5,1},{9,5},{13... | collective-permute-start | bytes 786440 | tf_op jit(solution)/shard_map/while/body/eval_jaxpr/ppermute | solution.py:27
  354.1 10.7 %collective-permute-start.5 = (f32[8,2,8,512]{3,0,2,1:T(8,128)S(1)}, f32[8,2,8,512]{3,0,2,1:T(8,128)S(1)}, u32[]{:S(2)}, u32[]{:S(2)}) collective-permute-start(f32[8,2,8,512]{3,0,2,1:T(8,128)S(1)} %get-tuple-element.874), channel_id=1, source_target_pairs={{4,0},{8,4},{12,8},{16,12},{20,16},{24,20},{28,24},{5,1},{9,5},{13... | collective-permute-start | bytes 786440 | tf_op jit(solution)/shard_map/while/body/eval_jaxpr/ppermute | solution.py:27
  376.8 10.7 %collective-permute-start.5 = (f32[8,2,8,512]{3,0,2,1:T(8,128)S(1)}, f32[8,2,8,512]{3,0,2,1:T(8,128)S(1)}, u32[]{:S(2)}, u32[]{:S(2)}) collective-permute-start(f32[8,2,8,512]{3,0,2,1:T(8,128)S(1)} %get-tuple-element.874), channel_id=1, source_target_pairs={{4,0},{8,4},{12,8},{16,12},{20,16},{24,20},{28,24},{5,1},{9,5},{13... | collective-permute-start | bytes 786440 | tf_op jit(solution)/shard_map/while/body/eval_jaxpr/ppermute | solution.py:27
  399.4 10.7 %collective-permute-start.5 = (f32[8,2,8,512]{3,0,2,1:T(8,128)S(1)}, f32[8,2,8,512]{3,0,2,1:T(8,128)S(1)}, u32[]{:S(2)}, u32[]{:S(2)}) collective-permute-start(f32[8,2,8,512]{3,0,2,1:T(8,128)S(1)} %get-tuple-element.874), channel_id=1, source_target_pairs={{4,0},{8,4},{12,8},{16,12},{20,16},{24,20},{28,24},{5,1},{9,5},{13... | collective-permute-start | bytes 786440 | tf_op jit(solution)/shard_map/while/body/eval_jaxpr/ppermute | solution.py:27
  422.0 10.7 %collective-permute-start.5 = (f32[8,2,8,512]{3,0,2,1:T(8,128)S(1)}, f32[8,2,8,512]{3,0,2,1:T(8,128)S(1)}, u32[]{:S(2)}, u32[]{:S(2)}) collective-permute-start(f32[8,2,8,512]{3,0,2,1:T(8,128)S(1)} %get-tuple-element.874), channel_id=1, source_target_pairs={{4,0},{8,4},{12,8},{16,12},{20,16},{24,20},{28,24},{5,1},{9,5},{13... | collective-permute-start | bytes 786440 | tf_op jit(solution)/shard_map/while/body/eval_jaxpr/ppermute | solution.py:27
  444.6 10.7 %collective-permute-start.5 = (f32[8,2,8,512]{3,0,2,1:T(8,128)S(1)}, f32[8,2,8,512]{3,0,2,1:T(8,128)S(1)}, u32[]{:S(2)}, u32[]{:S(2)}) collective-permute-start(f32[8,2,8,512]{3,0,2,1:T(8,128)S(1)} %get-tuple-element.874), channel_id=1, source_target_pairs={{4,0},{8,4},{12,8},{16,12},{20,16},{24,20},{28,24},{5,1},{9,5},{13... | collective-permute-start | bytes 786440 | tf_op jit(solution)/shard_map/while/body/eval_jaxpr/ppermute | solution.py:27
  467.3 10.7 %collective-permute-start.5 = (f32[8,2,8,512]{3,0,2,1:T(8,128)S(1)}, f32[8,2,8,512]{3,0,2,1:T(8,128)S(1)}, u32[]{:S(2)}, u32[]{:S(2)}) collective-permute-start(f32[8,2,8,512]{3,0,2,1:T(8,128)S(1)} %get-tuple-element.874), channel_id=1, source_target_pairs={{4,0},{8,4},{12,8},{16,12},{20,16},{24,20},{28,24},{5,1},{9,5},{13... | collective-permute-start | bytes 786440 | tf_op jit(solution)/shard_map/while/body/eval_jaxpr/ppermute | solution.py:27
  (42 other events, 181.2 us)
